TPU v7x, 512 devices: a whole 4x4x16 slice. The times are simulated.
512 devices in a mesh: dom: 64 (over z, x_lo, core), bin: 8 (over y, x_hi).
Axes of the slice: x: 4 (x_hi: 2, x_lo: 2; x = x_hi * 2 + x_lo), y: 4, z: 16, core: 2. Of those that a mesh axis runs over, the one named last changes fastest.
Arguments:
- dust_rho: float32 [128, 65536], P('bin', 'dom'), may hold values from 0.25 to 4
- dust_vel: float32 [2, 128, 65536], P(None, 'bin', 'dom'), may hold values from -4 to 4
- gas_rho: float32 [65536], P('dom'), may hold values from 50 to 500
- gas_vel: float32 [2, 65536], P(None, 'dom'), may hold values from -4 to 4
- normals: float32 [2, 8, 65536], P(None, None, 'dom'), may hold values from -0.24 to 0.24
- inv_volume: float32 [65536], P('dom'), may hold values from 0.75 to 3
- coag_rate: float32 [65536], P('dom'), may hold values from 0.03 to 0.3
- drag_coef: float32 [128], P('bin'), as said below
- neighbours: int32 [8, 65536], P(None, 'dom'), may hold values from -1 to 1535, as said below
- send_cells: int32 [64, 4, 128], P('dom'), may hold values from -1 to 1023, as said below
- kernel: bfloat16 [128, 128], replicated, may hold values from 0.001953125 to 0.0703125, as said below
- redistrib: bfloat16 [128, 128], replicated, may hold values from -0.5 to 0.5
Outputs:
- dust_rho_out: float32 [128, 65536], P('bin', 'dom')
- dust_vel_out: float32 [2, 128, 65536], P(None, 'bin', 'dom')
- gas_vel_out: float32 [2, 65536], P(None, 'dom')
Inputs may be any that keep to these rules, and one draw needn't show every extreme that they name: Row send_cells[d, j] lists distinct cells of domain d, then -1 in the remaining slots; every row has 32 or more cells, and all rows of some domain are full. `neighbours`: an entry is -1, another local cell of the same domain, or 1024 + j * 128 + p for a ghost slot p that the sending domain fills; slot 0 of every cell is valid. `drag_coef`: Positive. `kernel`: positive and symmetric.
All inputs are finite; a program needn't handle non-finite values.
Results may differ from a plain program's by a relative error of at most 0.0048.
Values may be sent and summed in bfloat16 or wider, within the bound.
A program may use at most 64 MiB of HBM per device.

v0:
```python
import jax
import jax.numpy as jnp
from jax import lax
from jax.sharding import PartitionSpec as P

OFFSETS = (1, -1, 2, -2)


def from_behind(value, axis, steps):
    count = lax.axis_size(axis)
    pairs = [(source, (source + steps) % count) for source in range(count)]
    return lax.ppermute(value, axis, pairs)


def minmod(first, second):
    return 0.5 * (jnp.sign(first) + jnp.sign(second)) * jnp.minimum(jnp.abs(first), jnp.abs(second))


def advect(state, extended_rows, faces, face_normals, inv_vol):
    density = state[0]
    vel_x = state[1]
    vel_y = state[2]
    bin_rows = density.shape[0]
    cell_count = density.shape[1]
    face_count = faces.shape[0]
    valid_all = faces >= 0
    safe_all = jnp.maximum(faces, 0).reshape(face_count * cell_count)
    picked = jnp.take(extended_rows, safe_all, axis=0)
    picked = picked.reshape(face_count, cell_count, 3, bin_rows)
    picked = jnp.transpose(picked, (0, 2, 3, 1))
    total_mean = jnp.zeros_like(density)
    valid_count = jnp.zeros(density.shape[1:], jnp.float32)
    for face in range(face_count):
        valid = valid_all[face]
        total_mean = total_mean + jnp.where(valid, picked[face, 0], 0.0)
        valid_count = valid_count + valid.astype(jnp.float32)
    neighbour_mean = total_mean / valid_count
    flux_total = jnp.zeros_like(density)
    for face in range(face_count):
        valid = valid_all[face]
        other = picked[face, 0]
        speed = 0.5 * (
            (vel_x + picked[face, 1]) * face_normals[0, face]
            + (vel_y + picked[face, 2]) * face_normals[1, face]
        )
        limited = minmod(other - density, density - neighbour_mean)
        flux = jnp.maximum(speed, 0.0) * (density + 0.5 * limited) + jnp.minimum(speed, 0.0) * (
            other - 0.5 * limited
        )
        flux_total = flux_total + jnp.where(valid, flux, 0.0)
    return density - inv_vol * flux_total


def body(
    dust_rho,
    dust_vel,
    gas_rho,
    gas_vel,
    normals,
    inv_volume,
    coag_rate,
    drag_coef,
    neighbours,
    send_cells,
    kernel,
    redistrib,
):
    own_rows = dust_rho.shape[0]
    cell_count = dust_rho.shape[1]
    coupling = drag_coef[:, None] * gas_rho[None, :]
    share = coupling / (1.0 + coupling)
    weight = dust_rho / gas_rho[None, :] * share
    partial_sums = jnp.stack(
        [
            jnp.sum(weight, axis=0),
            jnp.sum(weight * dust_vel[0], axis=0),
            jnp.sum(weight * dust_vel[1], axis=0),
        ]
    )
    totals = lax.psum(partial_sums, "bin")
    gas_new = (gas_vel + totals[1:]) / (1.0 + totals[0])
    dust_vel_new = (dust_vel + coupling[None] * gas_new[:, None, :]) / (1.0 + coupling[None])
    state = jnp.concatenate([dust_rho[None], dust_vel_new], axis=0)
    state_rows = jnp.transpose(state.reshape(3 * own_rows, cell_count))
    blocks = [state_rows]
    for direction, offset in enumerate(OFFSETS):
        index = send_cells[0, direction]
        chosen = (
            jnp.take(state_rows, jnp.maximum(index, 0), axis=0)
            * (index >= 0).astype(jnp.float32)[:, None]
        )
        blocks.append(from_behind(chosen, "dom", offset))
    extended_rows = jnp.concatenate(blocks, axis=0)
    moved = advect(state, extended_rows, neighbours, normals, inv_volume)
    rounded = moved.astype(jnp.bfloat16)
    first_bin = lax.axis_index("bin") * own_rows
    kernel_rows = lax.dynamic_slice_in_dim(kernel, first_bin, own_rows, 0)
    columns = kernel_rows
    collide = jnp.dot(
        columns,
        lax.all_gather(rounded, "bin", axis=0, tiled=True),
        preferred_element_type=jnp.float32,
    )
    loss = (coag_rate[None, :] * rounded.astype(jnp.float32) * collide).astype(jnp.bfloat16)
    redis_rows = lax.dynamic_slice_in_dim(redistrib, first_bin, own_rows, 0)
    columns = redis_rows
    gain = jnp.dot(
        columns, lax.all_gather(loss, "bin", axis=0, tiled=True), preferred_element_type=jnp.float32
    )
    dust_rho_out = moved - loss.astype(jnp.float32) + gain
    return (dust_rho_out, dust_vel_new, gas_new)


def solution(mesh):
    placed = (
        P("bin", "dom"),
        P(None, "bin", "dom"),
        P("dom"),
        P(None, "dom"),
        P(None, None, "dom"),
        P("dom"),
        P("dom"),
        P("bin"),
        P(None, "dom"),
        P("dom", None, None),
        P(),
        P(),
    )
    return jax.shard_map(
        body,
        mesh=mesh,
        in_specs=placed,
        out_specs=(P("bin", "dom"), P(None, "bin", "dom"), P(None, "dom")),
        check_vma=False,
    )
```

profile of v0, /device:TPU:98, one launch (start us, length us, event | category | flops | bytes accessed | tf_op | source)
XLA Modules:
  0.0 177.4 jit_solution(4021776785599090148)
XLA Ops:
  0.6 0.8 compare_and_fusion
  1.5 0.8 fusion.65
  2.3 1.0 broadcast_multiply_fusion
  3.3 0.9 fusion.51
  4.2 41.3 %psum.7 = f32[3,1024]{1,0:T(4,128)S(1)} all-reduce(f32[3,1024]{1,0:T(4,128)S(1)} %pad_maximum_fusion.1), channel_id=1, replica_groups=mesh['dom'=64,'bin'=8] {'bin'}, use_global_device_ids=true, to_apply=%region_3.0 | all-reduce | flops 3072 | bytes 24576 | tf_op jit(solution)/shard_map/psum | solution.py:80
  45.5 0.7 fusion.52
  46.2 0.9 add_divide_fusion
  47.2 0.9 pad_maximum_fusion
  48.1 0.2 copy.28
  48.3 0.6 gather_fusion.1
  48.9 0.1 select_multiply_fusion.3
  49.0 1.9 %collective-permute-start = (f32[128,48]{1,0:T(8,128)S(1)}, f32[128,48]{1,0:T(8,128)S(1)}, u32[]{:S(2)}, u32[]{:S(2)}) collective-permute-start(f32[128,48]{1,0:T(8,128)S(1)} %select_multiply_fusion.3), channel_id=1, source_target_pairs={{0,8},{8,16},{16,24},{24,32},{32,40},{40,48},{48,56},{56,64},{64,7... | collective-permute-start | bytes 73736 | tf_op jit(solution)/shard_map/ppermute | solution.py:12
  51.0 0.6 gather_fusion.2
  51.6 0.1 select_multiply_fusion.2
  51.7 3.6 %collective-permute-start.1 = (f32[128,48]{1,0:T(8,128)S(1)}, f32[128,48]{1,0:T(8,128)S(1)}, u32[]{:S(2)}, u32[]{:S(2)}) collective-permute-start(f32[128,48]{1,0:T(8,128)S(1)} %select_multiply_fusion.2), channel_id=1, source_target_pairs={{0,504},{8,0},{16,8},{24,16},{32,24},{40,32},{48,40},{56,48},{64,5... | collective-permute-start | bytes 73736 | tf_op jit(solution)/shard_map/ppermute | solution.py:12
  55.4 0.6 gather_fusion.3
  56.1 0.1 select_multiply_fusion.1
  56.2 8.0 %collective-permute-start.2 = (f32[128,48]{1,0:T(8,128)S(1)}, f32[128,48]{1,0:T(8,128)S(1)}, u32[]{:S(2)}, u32[]{:S(2)}) collective-permute-start(f32[128,48]{1,0:T(8,128)S(1)} %select_multiply_fusion.1), channel_id=1, source_target_pairs={{0,16},{8,24},{16,32},{24,40},{32,48},{40,56},{48,64},{56,72},{64,... | collective-permute-start | bytes 73736 | tf_op jit(solution)/shard_map/ppermute | solution.py:12
  64.2 0.6 gather_fusion.4
  64.8 0.1 select_multiply_fusion
  65.0 1.9 %collective-permute-start.3 = (f32[128,48]{1,0:T(8,128)S(1)}, f32[128,48]{1,0:T(8,128)S(1)}, u32[]{:S(2)}, u32[]{:S(2)}) collective-permute-start(f32[128,48]{1,0:T(8,128)S(1)} %select_multiply_fusion), channel_id=1, source_target_pairs={{0,496},{8,504},{16,0},{24,8},{32,16},{40,24},{48,32},{56,40},{64,... | collective-permute-start | bytes 73736 | tf_op jit(solution)/shard_map/ppermute | solution.py:12
  67.2 0.1 slice_reduce_fusion.7
  67.4 5.9 %collective-permute-done.3 = f32[128,48]{1,0:T(8,128)S(1)} collective-permute-done((f32[128,48]{1,0:T(8,128)S(1)}, f32[128,48]{1,0:T(8,128)S(1)}, u32[]{:S(2)}, u32[]{:S(2)}) %collective-permute-start.3) | collective-permute-done | bytes 24608 | tf_op jit(solution)/shard_map/ppermute | solution.py:12
  73.2 27.7 %gather_fusion = f32[8192,48]{1,0:T(8,128)} fusion(f32[1536,48]{1,0:T(8,128)S(1)} %constant_dynamic-update-slice_fusion, s32[8192]{0:T(1024)S(1)} %broadcast_clamp_fusion), kind=kCustom, calls=%fused_computation.4 | custom fusion | bytes 3178496 | tf_op jit(solution)/shard_map/jit(_take)/gather | solution.py:28
  100.9 2.8 %copy.29 = f32[8192,48]{0,1:T(8,128)S(1)} copy(f32[8192,48]{1,0:T(8,128)} %gather_fusion) | data formatting | bytes 3145728 | tf_op jit(solution)/shard_map/jit(_take)/gather | solution.py:28
  103.7 0.9 copy.32
  104.7 1.0 fusion
  105.7 0.6 fusion.68
  106.4 34.8 %all_gather.6 = bf16[128,1024]{1,0:T(8,128)(2,1)S(1)} all-gather(bf16[16,1024]{1,0:T(8,128)(2,1)S(1)} %get-tuple-element.15), channel_id=1, replica_groups=mesh['dom'=64,'bin'=8] {'bin'}, dimensions={0}, use_global_device_ids=true | all-gather | bytes 294912 | tf_op jit(solution)/shard_map/all_gather | solution.py:101
  141.1 0.2 fusion.1
  141.3 34.7 %all_gather.7 = bf16[128,1024]{1,0:T(8,128)(2,1)S(1)} all-gather(bf16[16,1024]{1,0:T(8,128)(2,1)S(1)} %fusion.1), channel_id=1, replica_groups=mesh['dom'=64,'bin'=8] {'bin'}, dimensions={0}, use_global_device_ids=true | all-gather | bytes 294912 | tf_op jit(solution)/shard_map/all_gather | solution.py:108
  175.9 1.5 convolution_add_fusion
  (37 shorter events, 0.4 us)
Async XLA Ops:
  0.6 140.5 %copy-start = (bf16[128,128]{1,0:T(8,128)(2,1)S(1)}, bf16[128,128]{1,0:T(8,128)(2,1)}, u32[]{:S(2)}) copy-start(bf16[128,128]{1,0:T(8,128)(2,1)} %param.24) | copy-start | bytes 98308
  46.2 9.9 %copy-start.5 = (f32[2,1024]{1,0:T(2,128)}, f32[2,1024]{1,0:T(2,128)S(1)}, u32[]{:S(2)}) copy-start(f32[2,1024]{1,0:T(2,128)S(1)} %fusion.52) | copy-start | bytes 24580
  47.1 58.6 %copy-start.1 = (f32[2,16,1024]{2,1,0:T(8,128)}, f32[2,16,1024]{2,1,0:T(8,128)S(1)}, u32[]{:S(2)}) copy-start(f32[2,16,1024]{2,1,0:T(8,128)S(1)} %add_divide_fusion) | copy-start | bytes 393220
  49.0 18.3 %collective-permute-start = (f32[128,48]{1,0:T(8,128)S(1)}, f32[128,48]{1,0:T(8,128)S(1)}, u32[]{:S(2)}, u32[]{:S(2)}) collective-permute-start(f32[128,48]{1,0:T(8,128)S(1)} %select_multiply_fusion.3), channel_id=1, source_target_pairs={{0,8},{8,16},{16,24},{24,32},{32,40},{40,48},{48,56},{56,64},{64,7... | collective-permute-start | bytes 73736 | tf_op jit(solution)/shard_map/ppermute | solution.py:12
  51.0 16.0 %copy-start.3 = (s32[8,1024]{1,0:T(8,128)S(1)}, s32[8,1024]{1,0:T(8,128)}, u32[]{:S(2)}) copy-start(s32[8,1024]{1,0:T(8,128)} %param.22) | copy-start | bytes 98308
  51.6 15.4 %copy-start.4 = (f32[2,8,1024]{2,1,0:T(8,128)S(1)}, f32[2,8,1024]{2,1,0:T(8,128)}, u32[]{:S(2)}) copy-start(f32[2,8,1024]{2,1,0:T(8,128)} %param.18) | copy-start | bytes 196612
  51.7 15.6 %collective-permute-start.1 = (f32[128,48]{1,0:T(8,128)S(1)}, f32[128,48]{1,0:T(8,128)S(1)}, u32[]{:S(2)}, u32[]{:S(2)}) collective-permute-start(f32[128,48]{1,0:T(8,128)S(1)} %select_multiply_fusion.2), channel_id=1, source_target_pairs={{0,504},{8,0},{16,8},{24,16},{32,24},{40,32},{48,40},{56,48},{64,5... | collective-permute-start | bytes 73736 | tf_op jit(solution)/shard_map/ppermute | solution.py:12
  56.2 11.2 %collective-permute-start.2 = (f32[128,48]{1,0:T(8,128)S(1)}, f32[128,48]{1,0:T(8,128)S(1)}, u32[]{:S(2)}, u32[]{:S(2)}) collective-permute-start(f32[128,48]{1,0:T(8,128)S(1)} %select_multiply_fusion.1), channel_id=1, source_target_pairs={{0,16},{8,24},{16,32},{24,40},{32,48},{40,56},{48,64},{56,72},{64,... | collective-permute-start | bytes 73736 | tf_op jit(solution)/shard_map/ppermute | solution.py:12
  65.0 8.3 %collective-permute-start.3 = (f32[128,48]{1,0:T(8,128)S(1)}, f32[128,48]{1,0:T(8,128)S(1)}, u32[]{:S(2)}, u32[]{:S(2)}) collective-permute-start(f32[128,48]{1,0:T(8,128)S(1)} %select_multiply_fusion), channel_id=1, source_target_pairs={{0,496},{8,504},{16,0},{24,8},{32,16},{40,24},{48,32},{56,40},{64,... | collective-permute-start | bytes 73736 | tf_op jit(solution)/shard_map/ppermute | solution.py:12
  104.6 1.1 copy-start.2
  104.7 1.1 copy-start.6
  105.7 35.4 %copy-start.7 = (f32[1024]{0:T(1024)S(1)}, f32[1024]{0:T(1024)}, u32[]{:S(2)}) copy-start(f32[1024]{0:T(1024)} %param.20) | copy-start | bytes 12292
where the time goes:
time: 178 us; the launch traced here: 177 us
  blocking collectives  111 us (62%)
  local copies, waits for them, and re-layouts  34.5 us (19%)
  starting transfers between devices  15.5 us (9%)
  other arithmetic  8.26 us (5%)
  waiting for transfers between devices  5.86 us (3%)
    psum x1, blocking collectives, body(): totals = lax.psum(partial_sums, 'bin')  41.3 us
    all_gather x1, blocking collectives, body(): lax.all_gather(rounded, 'bin', axis=0, tiled=True)  34.8 us
    all_gather x1, blocking collectives, body(): lax.all_gather(loss, 'bin', axis=0, tiled=True)  34.7 us
    gather x2, local copies, waits for them, and re-layouts, advect(): picked = jnp.take(extended_rows, safe_all, axis=0)  30.5 us
    ppermute x4, starting transfers between devices, from_behind(): return lax.ppermute(value, axis, pairs)  15.5 us
    ppermute x4, waiting for transfers between devices, from_behind(): return lax.ppermute(value, axis, pairs)  5.86 us
  transfers between devices with their start and end apart: 4, of which 1 were waited for; matrix products, arithmetic and copies ran while one was open for 1% of the time, Pallas kernels for 0%

commit v1 on v0

v1 whole, which is shorter than its diff:
```python
import jax
import jax.numpy as jnp
from jax import lax
from jax.experimental import pallas as pl
from jax.experimental.pallas import tpu as pltpu
from jax.sharding import PartitionSpec as P

OFFSETS = (1, -1, 2, -2)
LANES = 128
SUB = 8
MESH = pl.DeviceIdType.MESH


def spread(row):
    return jnp.broadcast_to(row, (SUB, LANES))


def lane_take(block, lanes):
    return jnp.take_along_axis(block, lanes, axis=1, mode="promise_in_bounds")


def minmod(first, second):
    return jnp.maximum(jnp.minimum(first, second), 0.0) + jnp.minimum(
        jnp.maximum(first, second), 0.0
    )


def kernel_body(
    bins,
    doms,
    rho_ref,
    vel_ref,
    gas_rho_ref,
    gas_vel_ref,
    normals_ref,
    inv_ref,
    coag_ref,
    drag_ref,
    faces_ref,
    send_ref,
    kern_ref,
    redis_ref,
    rho_out,
    vel_out,
    gas_out,
    ext,
    picked,
    sums,
    ghost_out,
    moved,
    rounded,
    mixed,
    delta,
    back,
    sum_send,
    sum_recv,
    rho_send,
    rho_recv,
    vel_send,
    vel_recv,
    mix_send,
    mix_recv,
    back_send,
    back_recv,
):
    rows = rho_ref.shape[0]
    groups = rho_ref.shape[1] // LANES
    face_count = faces_ref.shape[0]
    halves = rows // SUB
    me = lax.axis_index("bin")
    dom = lax.axis_index("dom")

    barrier = pltpu.get_barrier_semaphore()
    for step in range(1, bins):
        pl.semaphore_signal(
            barrier, inc=1, device_id={"bin": lax.rem(me + step, bins)}, device_id_type=MESH
        )
    for offset in OFFSETS:
        pl.semaphore_signal(
            barrier,
            inc=1,
            device_id={"dom": lax.rem(dom + offset + doms, doms)},
            device_id_type=MESH,
        )

    diagonal = lax.broadcasted_iota(jnp.int32, (rows, rows), 0) == lax.broadcasted_iota(
        jnp.int32, (rows, rows), 1
    )
    drag = jnp.sum(
        jnp.where(diagonal, jnp.broadcast_to(drag_ref[...], (rows, rows)), 0.0),
        axis=1,
        keepdims=True,
    )

    for c in range(groups):
        cells = slice(c * LANES, (c + 1) * LANES)
        density = rho_ref[:, cells]
        ext[c, 0:rows, :] = density
        gas_rho = gas_rho_ref[c : c + 1, :]
        coupling = drag * gas_rho
        weight = density / gas_rho * (coupling / (1.0 + coupling))
        sums[me, 0, c : c + 1, :] = jnp.sum(weight, axis=0, keepdims=True)
        sums[me, 1, c : c + 1, :] = jnp.sum(weight * vel_ref[0, :, cells], axis=0, keepdims=True)
        sums[me, 2, c : c + 1, :] = jnp.sum(weight * vel_ref[1, :, cells], axis=0, keepdims=True)

    def choose(first_row, last_row):
        for j in range(len(OFFSETS)):
            index = spread(send_ref[j : j + 1, :])
            safe = jnp.maximum(index, 0)
            lanes = safe & (LANES - 1)
            block = safe >> 7
            for r in range(first_row, last_row, SUB):
                value = lane_take(ext[0, r : r + SUB, :], lanes)
                for s in range(1, groups):
                    value = jnp.where(
                        block == s, lane_take(ext[s, r : r + SUB, :], lanes), value
                    )
                ghost_out[j, r : r + SUB, :] = jnp.where(index >= 0, value, 0.0)

    def ghost_copy(j, first_row, last_row, send_sem, recv_sem):
        return pltpu.make_async_remote_copy(
            src_ref=ghost_out.at[j, first_row:last_row],
            dst_ref=ext.at[groups + j, first_row:last_row],
            send_sem=send_sem.at[j],
            recv_sem=recv_sem.at[j],
            device_id={"dom": lax.rem(dom + OFFSETS[j] + doms, doms)},
            device_id_type=MESH,
        )

    choose(0, rows)
    pl.semaphore_wait(barrier, bins - 1 + len(OFFSETS))

    def peer_copy(step, source, target, send_sem, recv_sem):
        return pltpu.make_async_remote_copy(
            src_ref=source,
            dst_ref=target,
            send_sem=send_sem.at[step],
            recv_sem=recv_sem.at[step],
            device_id={"bin": lax.rem(me + step, bins)},
            device_id_type=MESH,
        )

    def peer_arrived(step, source, buffer, send_sem, recv_sem):
        sender = lax.rem(me + bins - step, bins)
        peer_copy(step, source, buffer.at[sender], send_sem, recv_sem).wait_recv()

    for step in range(1, bins):
        peer_copy(step, sums.at[me], sums.at[me], sum_send, sum_recv).start()
    for j in range(len(OFFSETS)):
        ghost_copy(j, 0, rows, rho_send, rho_recv).start()

    def pick(first_block, last_block, first_row, last_row):
        def group(c, carry):
            cells = pl.ds(pl.multiple_of(c * LANES, LANES), LANES)
            for k in range(face_count):
                safe = jnp.maximum(spread(faces_ref[k : k + 1, cells]), 0)
                lanes = safe & (LANES - 1)
                block = safe >> 7
                for r in range(first_row, last_row, SUB):
                    if first_block == 0:
                        value = lane_take(ext[0, r : r + SUB, :], lanes)
                    else:
                        value = picked[c, k, r : r + SUB, :]
                    for s in range(max(first_block, 1), last_block):
                        value = jnp.where(
                            block == s, lane_take(ext[s, r : r + SUB, :], lanes), value
                        )
                    picked[c, k, r : r + SUB, :] = value
            return carry

        lax.fori_loop(0, groups, group, 0)

    total_blocks = groups + len(OFFSETS)
    pick(0, groups, 0, rows)
    for j in range(len(OFFSETS)):
        ghost_copy(j, 0, rows, rho_send, rho_recv).wait_recv()
    pick(groups, total_blocks, 0, rows)

    for step in range(1, bins):
        peer_arrived(step, sums.at[me], sums, sum_send, sum_recv)
    totals = sums[0]
    for b in range(1, bins):
        totals = totals + sums[b]

    for c in range(groups):
        cells = slice(c * LANES, (c + 1) * LANES)
        scale = 1.0 + totals[0, c : c + 1, :]
        coupling = drag * gas_rho_ref[c : c + 1, :]
        for component in range(2):
            gas = (
                gas_vel_ref[component : component + 1, cells]
                + totals[component + 1, c : c + 1, :]
            ) / scale
            gas_out[component : component + 1, cells] = gas
            dust = (vel_ref[component, :, cells] + coupling * gas) / (1.0 + coupling)
            vel_out[component, :, cells] = dust
            ext[c, (component + 1) * rows : (component + 2) * rows, :] = dust

    choose(rows, 3 * rows)
    for j in range(len(OFFSETS)):
        ghost_copy(j, rows, 3 * rows, vel_send, vel_recv).start()
    pick(0, groups, rows, 3 * rows)
    for j in range(len(OFFSETS)):
        ghost_copy(j, rows, 3 * rows, vel_send, vel_recv).wait_recv()
    pick(groups, total_blocks, rows, 3 * rows)

    def advect(c, carry):
        cells = pl.ds(pl.multiple_of(c * LANES, LANES), LANES)
        valid = [spread(faces_ref[k : k + 1, cells]) >= 0 for k in range(face_count)]
        count = valid[0].astype(jnp.float32)
        for k in range(1, face_count):
            count = count + valid[k].astype(jnp.float32)
        inverse = spread(inv_ref[pl.ds(c, 1), :])
        for h in range(halves):
            first = slice(h * SUB, (h + 1) * SUB)
            second = slice(rows + h * SUB, rows + (h + 1) * SUB)
            third = slice(2 * rows + h * SUB, 2 * rows + (h + 1) * SUB)
            density = ext[c, first, :]
            vel_x = ext[c, second, :]
            vel_y = ext[c, third, :]
            mean = jnp.where(valid[0], picked[c, 0, first, :], 0.0)
            for k in range(1, face_count):
                mean = mean + jnp.where(valid[k], picked[c, k, first, :], 0.0)
            slope = density - mean / count
            total = jnp.zeros((SUB, LANES), jnp.float32)
            for k in range(face_count):
                other = picked[c, k, first, :]
                speed = 0.5 * (
                    (vel_x + picked[c, k, second, :]) * spread(normals_ref[0, k : k + 1, cells])
                    + (vel_y + picked[c, k, third, :]) * spread(normals_ref[1, k : k + 1, cells])
                )
                limited = 0.5 * minmod(other - density, slope)
                flux = jnp.maximum(speed, 0.0) * (density + limited) + jnp.minimum(speed, 0.0) * (
                    other - limited
                )
                total = total + jnp.where(valid[k], flux, 0.0)
            moved[c, first, :] = density - inverse * total
        rounded[c] = moved[c].astype(jnp.bfloat16)
        return carry

    lax.fori_loop(0, groups, advect, 0)

    for step in range(1, bins):
        peer = lax.rem(me + step, bins)
        peer_copy(step, rounded.at[peer], mixed.at[me], mix_send, mix_recv).start()
    mixed[me] = rounded[me]
    for step in range(1, bins):
        peer_arrived(step, rounded.at[0], mixed, mix_send, mix_recv)
    columns = mixed[...].reshape(bins * rows, LANES)
    collide = jnp.dot(kern_ref[...], columns, preferred_element_type=jnp.float32)
    rate = coag_ref[pl.ds(me, 1), :]
    loss = (rate * columns.astype(jnp.float32) * collide).astype(jnp.bfloat16)
    gain = jnp.dot(redis_ref[...], loss, preferred_element_type=jnp.float32)
    delta[...] = (gain - loss.astype(jnp.float32)).reshape(bins, rows, LANES)
    for step in range(1, bins):
        peer = lax.rem(me + step, bins)
        peer_copy(step, delta.at[peer], back.at[me], back_send, back_recv).start()
    back[me] = delta[me]
    for step in range(1, bins):
        peer_arrived(step, delta.at[0], back, back_send, back_recv)
    for c in range(groups):
        rho_out[:, c * LANES : (c + 1) * LANES] = moved[c] + back[c]

    for step in range(1, bins):
        peer = lax.rem(me + step, bins)
        peer_copy(step, sums.at[me], sums.at[me], sum_send, sum_recv).wait_send()
        peer_copy(step, rounded.at[peer], mixed.at[me], mix_send, mix_recv).wait_send()
        peer_copy(step, delta.at[peer], back.at[me], back_send, back_recv).wait_send()
    for j in range(len(OFFSETS)):
        ghost_copy(j, 0, rows, rho_send, rho_recv).wait_send()
        ghost_copy(j, rows, 3 * rows, vel_send, vel_recv).wait_send()


def body(
    dust_rho,
    dust_vel,
    gas_rho,
    gas_vel,
    normals,
    inv_volume,
    coag_rate,
    drag_coef,
    neighbours,
    send_cells,
    kernel,
    redistrib,
):
    rows, cells = dust_rho.shape
    bins = lax.axis_size("bin")
    doms = lax.axis_size("dom")
    groups = cells // LANES
    faces = neighbours.shape[0]
    ghosts = len(OFFSETS)

    def run(*refs):
        kernel_body(bins, doms, *refs)

    vmem = pl.BlockSpec(memory_space=pltpu.VMEM)
    dma = pltpu.SemaphoreType.DMA
    return pl.pallas_call(
        run,
        name="dust_step",
        out_shape=(
            jax.ShapeDtypeStruct(dust_rho.shape, jnp.float32),
            jax.ShapeDtypeStruct(dust_vel.shape, jnp.float32),
            jax.ShapeDtypeStruct(gas_vel.shape, jnp.float32),
        ),
        in_specs=[vmem] * 12,
        out_specs=(vmem, vmem, vmem),
        scratch_shapes=[
            pltpu.VMEM((groups + ghosts, 3 * rows, LANES), jnp.float32),
            pltpu.VMEM((groups, faces, 3 * rows, LANES), jnp.float32),
            pltpu.VMEM((bins, 3, groups, LANES), jnp.float32),
            pltpu.VMEM((ghosts, 3 * rows, LANES), jnp.float32),
            pltpu.VMEM((groups, rows, LANES), jnp.float32),
            pltpu.VMEM((groups, rows, LANES), jnp.bfloat16),
            pltpu.VMEM((bins, rows, LANES), jnp.bfloat16),
            pltpu.VMEM((bins, rows, LANES), jnp.float32),
            pltpu.VMEM((bins, rows, LANES), jnp.float32),
            dma((bins,)),
            dma((bins,)),
            dma((ghosts,)),
            dma((ghosts,)),
            dma((ghosts,)),
            dma((ghosts,)),
            dma((bins,)),
            dma((bins,)),
            dma((bins,)),
            dma((bins,)),
        ],
        compiler_params=pltpu.CompilerParams(collective_id=0, has_side_effects=True),
    )(
        dust_rho,
        dust_vel,
        gas_rho.reshape(groups, LANES),
        gas_vel,
        normals,
        inv_volume.reshape(groups, LANES),
        coag_rate.reshape(groups, LANES),
        drag_coef.reshape(1, rows),
        neighbours,
        send_cells.reshape(ghosts, LANES),
        kernel,
        redistrib,
    )


def solution(mesh):
    placed = (
        P("bin", "dom"),
        P(None, "bin", "dom"),
        P("dom"),
        P(None, "dom"),
        P(None, None, "dom"),
        P("dom"),
        P("dom"),
        P("bin"),
        P(None, "dom"),
        P("dom", None, None),
        P(),
        P(),
    )
    return jax.shard_map(
        body,
        mesh=mesh,
        in_specs=placed,
        out_specs=(P("bin", "dom"), P(None, "bin", "dom"), P(None, "dom")),
        check_vma=False,
    )
```

time: 178 us -> 40 us (0.22)
  the two profiles are of different devices: /device:TPU:98 before, /device:TPU:8 now
where the time goes in v1:
time: 40 us; the launch traced here: 39.8 us
  Pallas kernels  36.3 us (91%)
  local copies, waits for them, and re-layouts  2.81 us (7%)
  between operations  0.65 us (2%)
    pallas_call x1, Pallas kernels, body(): pl.pallas_call(run, name='dust_step', out_shape=(jax.ShapeDtypeStruct(dus...  36.3 us
    unnamed x7, local copies, waits for them, and re-layouts  2.81 us

profile of v1, /device:TPU:8, one launch (start us, length us, event | category | flops | bytes accessed | tf_op | source)
XLA Modules:
  0.0 39.8 jit_solution(12094289198465900806)
XLA Ops:
  0.6 36.3 %dust_step.1 = (f32[16,1024]{1,0:T(8,128)}, f32[2,16,1024]{2,1,0:T(8,128)}, f32[2,1024]{1,0:T(2,128)}) custom-call(f32[16,1024]{1,0:T(8,128)} %refs_0_.1, f32[2,16,1024]{2,1,0:T(8,128)} %refs_1_.1, f32[8,128]{1,0:T(8,128)} %bitcast.5, f32[2,1024]{1,0:T(2,128)} %refs_3_.1, f32[2,8,1024]{2,1,0:T(8,128)} %refs_4_.1, f32[8,128]{1,0:T(8,128)} %bitcast.6, ...), custom_call_target="tpu_custom_call" | custom-call | tf_op jit(solution)/shard_map/dust_step/pallas_call | solution.py:300
  36.9 0.0 copy-start
  36.9 1.5 %copy.18 = f32[16,1024]{1,0:T(8,128)} copy(f32[16,1024]{1,0:T(8,128)} %get-tuple-element.6) | data formatting | bytes 131072
  38.5 0.0 copy-done
  38.5 0.0 copy-start.1
  38.5 0.7 %copy.19 = f32[2,16,1024]{2,1,0:T(8,128)} copy(f32[2,16,1024]{2,1,0:T(8,128)S(1)} %copy-done) | data formatting | bytes 262144
  39.1 0.0 copy-done.1
  39.2 0.6 %copy.20 = f32[2,1024]{1,0:T(2,128)} copy(f32[2,1024]{1,0:T(2,128)S(1)} %copy-done.1) | data formatting | bytes 16384
Async XLA Ops:
  36.9 1.5 %copy-start = (f32[2,16,1024]{2,1,0:T(8,128)S(1)}, f32[2,16,1024]{2,1,0:T(8,128)}, u32[]{:S(2)}) copy-start(f32[2,16,1024]{2,1,0:T(8,128)} %get-tuple-element.7) | copy-start | bytes 393220
  38.5 0.7 %copy-start.1 = (f32[2,1024]{1,0:T(2,128)S(1)}, f32[2,1024]{1,0:T(2,128)}, u32[]{:S(2)}) copy-start(f32[2,1024]{1,0:T(2,128)} %get-tuple-element.8) | copy-start | bytes 24580

commit v2 on v1

--- a/solution.py
+++ b/solution.py
@@ -9,6 +9,9 @@
 LANES = 128
 SUB = 8
 MESH = pl.DeviceIdType.MESH
+STEPS = 8191.0
+MIDDLE = 32768.0
+UNROLL = 4
 
 
 def spread(row):
@@ -17,6 +20,12 @@
 
 def lane_take(block, lanes):
     return jnp.take_along_axis(block, lanes, axis=1, mode="promise_in_bounds")
+
+
+def join(vel_x, vel_y):
+    first = (vel_x * STEPS + (MIDDLE + 0.5)).astype(jnp.int32)
+    second = (vel_y * STEPS + (MIDDLE + 0.5)).astype(jnp.int32)
+    return first * 65536 + second
 
 
 def minmod(first, second):
@@ -28,41 +37,49 @@
 def kernel_body(
     bins,
     doms,
-    rho_ref,
-    vel_ref,
-    gas_rho_ref,
-    gas_vel_ref,
-    normals_ref,
-    inv_ref,
-    coag_ref,
-    drag_ref,
-    faces_ref,
-    send_ref,
-    kern_ref,
-    redis_ref,
-    rho_out,
-    vel_out,
-    gas_out,
-    ext,
-    picked,
-    sums,
-    ghost_out,
-    moved,
-    rounded,
-    mixed,
-    delta,
-    back,
-    sum_send,
-    sum_recv,
-    rho_send,
-    rho_recv,
-    vel_send,
-    vel_recv,
-    mix_send,
-    mix_recv,
-    back_send,
-    back_recv,
+    *refs,
 ):
+    held = refs[:12]
+    rho_out, vel_out, gas_out = refs[12:15]
+    inputs = refs[15:27]
+    loaded = refs[27]
+    (
+        rho_ref,
+        vel_ref,
+        gas_rho_ref,
+        gas_vel_ref,
+        normals_ref,
+        inv_ref,
+        coag_ref,
+        drag_ref,
+        faces_ref,
+        send_ref,
+        kern_ref,
+        redis_ref,
+    ) = inputs
+    (
+        ext,
+        coded,
+        picked,
+        picked_vel,
+        sums,
+        ghost_out,
+        moved,
+        rounded,
+        mixed,
+        delta,
+        back,
+        sum_send,
+        sum_recv,
+        rho_send,
+        rho_recv,
+        vel_send,
+        vel_recv,
+        mix_send,
+        mix_recv,
+        back_send,
+        back_recv,
+    ) = refs[28:]
     rows = rho_ref.shape[0]
     groups = rho_ref.shape[1] // LANES
     face_count = faces_ref.shape[0]
@@ -82,6 +99,14 @@
             device_id={"dom": lax.rem(dom + offset + doms, doms)},
             device_id_type=MESH,
         )
+
+    loads = [
+        pltpu.make_async_copy(held[i], inputs[i], loaded.at[i]) for i in range(len(inputs))
+    ]
+    for i in (0, 2, 7, 9, 1, 8, 3, 4, 5, 6, 10, 11):
+        loads[i].start()
+    for i in (0, 2, 7, 1):
+        loads[i].wait()
 
     diagonal = lax.broadcasted_iota(jnp.int32, (rows, rows), 0) == lax.broadcasted_iota(
         jnp.int32, (rows, rows), 1
@@ -127,6 +152,7 @@
             device_id_type=MESH,
         )
 
+    loads[9].wait()
     choose(0, rows)
     pl.semaphore_wait(barrier, bins - 1 + len(OFFSETS))
 
@@ -149,32 +175,39 @@
     for j in range(len(OFFSETS)):
         ghost_copy(j, 0, rows, rho_send, rho_recv).start()
 
-    def pick(first_block, last_block, first_row, last_row):
-        def group(c, carry):
-            cells = pl.ds(pl.multiple_of(c * LANES, LANES), LANES)
-            for k in range(face_count):
-                safe = jnp.maximum(spread(faces_ref[k : k + 1, cells]), 0)
-                lanes = safe & (LANES - 1)
-                block = safe >> 7
-                for r in range(first_row, last_row, SUB):
-                    if first_block == 0:
-                        value = lane_take(ext[0, r : r + SUB, :], lanes)
-                    else:
-                        value = picked[c, k, r : r + SUB, :]
-                    for s in range(max(first_block, 1), last_block):
-                        value = jnp.where(
-                            block == s, lane_take(ext[s, r : r + SUB, :], lanes), value
-                        )
-                    picked[c, k, r : r + SUB, :] = value
+    def pick(first_block, last_block, source, target, c, faces):
+        cells = pl.ds(pl.multiple_of(c * LANES, LANES), LANES)
+        for k in faces:
+            safe = jnp.maximum(spread(faces_ref[k : k + 1, cells]), 0)
+            lanes = safe & (LANES - 1)
+            block = safe >> 7
+            for r in range(0, rows, SUB):
+                if first_block == 0:
+                    value = lane_take(source[0, r : r + SUB, :], lanes)
+                else:
+                    value = target[c, k, r : r + SUB, :]
+                for s in range(max(first_block, 1), last_block):
+                    value = jnp.where(
+                        block == s, lane_take(source[s, r : r + SUB, :], lanes), value
+                    )
+                target[c, k, r : r + SUB, :] = value
+
+    def pick_all(first_block, last_block, source, target):
+        def part(i, carry):
+            for u in range(UNROLL):
+                pick(first_block, last_block, source, target, i * UNROLL + u, range(face_count))
             return carry
 
-        lax.fori_loop(0, groups, group, 0)
+        lax.fori_loop(0, groups // UNROLL, part, 0)
 
     total_blocks = groups + len(OFFSETS)
-    pick(0, groups, 0, rows)
+    loads[8].wait()
+    pick_all(0, groups, ext, picked)
     for j in range(len(OFFSETS)):
         ghost_copy(j, 0, rows, rho_send, rho_recv).wait_recv()
-    pick(groups, total_blocks, 0, rows)
+    pick_all(groups, total_blocks, ext, picked)
+    for i in (3, 4, 5, 6, 10, 11):
+        loads[i].wait()
 
     for step in range(1, bins):
         peer_arrived(step, sums.at[me], sums, sum_send, sum_recv)
@@ -186,6 +219,7 @@
         cells = slice(c * LANES, (c + 1) * LANES)
         scale = 1.0 + totals[0, c : c + 1, :]
         coupling = drag * gas_rho_ref[c : c + 1, :]
+        both = []
         for component in range(2):
             gas = (
                 gas_vel_ref[component : component + 1, cells]
@@ -195,16 +229,21 @@
             dust = (vel_ref[component, :, cells] + coupling * gas) / (1.0 + coupling)
             vel_out[component, :, cells] = dust
             ext[c, (component + 1) * rows : (component + 2) * rows, :] = dust
+            both.append(dust)
+        coded[c] = join(both[0], both[1])
 
     choose(rows, 3 * rows)
     for j in range(len(OFFSETS)):
         ghost_copy(j, rows, 3 * rows, vel_send, vel_recv).start()
-    pick(0, groups, rows, 3 * rows)
+    pick_all(0, groups, coded, picked_vel)
     for j in range(len(OFFSETS)):
         ghost_copy(j, rows, 3 * rows, vel_send, vel_recv).wait_recv()
-    pick(groups, total_blocks, rows, 3 * rows)
-
-    def advect(c, carry):
+        coded[groups + j] = join(
+            ext[groups + j, rows : 2 * rows, :], ext[groups + j, 2 * rows : 3 * rows, :]
+        )
+
+    def advect(c):
+        pick(groups, total_blocks, coded, picked_vel, c, range(face_count))
         cells = pl.ds(pl.multiple_of(c * LANES, LANES), LANES)
         valid = [spread(faces_ref[k : k + 1, cells]) >= 0 for k in range(face_count)]
         count = valid[0].astype(jnp.float32)
@@ -216,8 +255,8 @@
             second = slice(rows + h * SUB, rows + (h + 1) * SUB)
             third = slice(2 * rows + h * SUB, 2 * rows + (h + 1) * SUB)
             density = ext[c, first, :]
-            vel_x = ext[c, second, :]
-            vel_y = ext[c, third, :]
+            vel_x = ext[c, second, :] - MIDDLE / STEPS
+            vel_y = ext[c, third, :] - MIDDLE / STEPS
             mean = jnp.where(valid[0], picked[c, 0, first, :], 0.0)
             for k in range(1, face_count):
                 mean = mean + jnp.where(valid[k], picked[c, k, first, :], 0.0)
@@ -225,9 +264,12 @@
             total = jnp.zeros((SUB, LANES), jnp.float32)
             for k in range(face_count):
                 other = picked[c, k, first, :]
+                pair = picked_vel[c, k, first, :]
+                other_x = lax.shift_right_logical(pair, 16).astype(jnp.float32) * (1.0 / STEPS)
+                other_y = (pair & 65535).astype(jnp.float32) * (1.0 / STEPS)
                 speed = 0.5 * (
-                    (vel_x + picked[c, k, second, :]) * spread(normals_ref[0, k : k + 1, cells])
-                    + (vel_y + picked[c, k, third, :]) * spread(normals_ref[1, k : k + 1, cells])
+                    (vel_x + other_x) * spread(normals_ref[0, k : k + 1, cells])
+                    + (vel_y + other_y) * spread(normals_ref[1, k : k + 1, cells])
                 )
                 limited = 0.5 * minmod(other - density, slope)
                 flux = jnp.maximum(speed, 0.0) * (density + limited) + jnp.minimum(speed, 0.0) * (
@@ -236,13 +278,15 @@
                 total = total + jnp.where(valid[k], flux, 0.0)
             moved[c, first, :] = density - inverse * total
         rounded[c] = moved[c].astype(jnp.bfloat16)
-        return carry
-
-    lax.fori_loop(0, groups, advect, 0)
-
-    for step in range(1, bins):
-        peer = lax.rem(me + step, bins)
-        peer_copy(step, rounded.at[peer], mixed.at[me], mix_send, mix_recv).start()
+
+    order = [(bins // 2 + turn) % bins for turn in (0, 1, 7, 3, 2, 5, 6, 4)]
+    for first in range(0, bins, UNROLL):
+        for step in order[first : first + UNROLL]:
+            advect(lax.rem(me + step, bins))
+        for step in order[first : first + UNROLL]:
+            if step > 0:
+                peer = lax.rem(me + step, bins)
+                peer_copy(step, rounded.at[peer], mixed.at[me], mix_send, mix_recv).start()
     mixed[me] = rounded[me]
     for step in range(1, bins):
         peer_arrived(step, rounded.at[0], mixed, mix_send, mix_recv)
@@ -295,41 +339,7 @@
     def run(*refs):
         kernel_body(bins, doms, *refs)
 
-    vmem = pl.BlockSpec(memory_space=pltpu.VMEM)
-    dma = pltpu.SemaphoreType.DMA
-    return pl.pallas_call(
-        run,
-        name="dust_step",
-        out_shape=(
-            jax.ShapeDtypeStruct(dust_rho.shape, jnp.float32),
-            jax.ShapeDtypeStruct(dust_vel.shape, jnp.float32),
-            jax.ShapeDtypeStruct(gas_vel.shape, jnp.float32),
-        ),
-        in_specs=[vmem] * 12,
-        out_specs=(vmem, vmem, vmem),
-        scratch_shapes=[
-            pltpu.VMEM((groups + ghosts, 3 * rows, LANES), jnp.float32),
-            pltpu.VMEM((groups, faces, 3 * rows, LANES), jnp.float32),
-            pltpu.VMEM((bins, 3, groups, LANES), jnp.float32),
-            pltpu.VMEM((ghosts, 3 * rows, LANES), jnp.float32),
-            pltpu.VMEM((groups, rows, LANES), jnp.float32),
-            pltpu.VMEM((groups, rows, LANES), jnp.bfloat16),
-            pltpu.VMEM((bins, rows, LANES), jnp.bfloat16),
-            pltpu.VMEM((bins, rows, LANES), jnp.float32),
-            pltpu.VMEM((bins, rows, LANES), jnp.float32),
-            dma((bins,)),
-            dma((bins,)),
-            dma((ghosts,)),
-            dma((ghosts,)),
-            dma((ghosts,)),
-            dma((ghosts,)),
-            dma((bins,)),
-            dma((bins,)),
-            dma((bins,)),
-            dma((bins,)),
-        ],
-        compiler_params=pltpu.CompilerParams(collective_id=0, has_side_effects=True),
-    )(
+    arrays = (
         dust_rho,
         dust_vel,
         gas_rho.reshape(groups, LANES),
@@ -343,6 +353,45 @@
         kernel,
         redistrib,
     )
+    vmem = pl.BlockSpec(memory_space=pltpu.VMEM)
+    dma = pltpu.SemaphoreType.DMA
+    return pl.pallas_call(
+        run,
+        name="dust_step",
+        out_shape=(
+            jax.ShapeDtypeStruct(dust_rho.shape, jnp.float32),
+            jax.ShapeDtypeStruct(dust_vel.shape, jnp.float32),
+            jax.ShapeDtypeStruct(gas_vel.shape, jnp.float32),
+        ),
+        in_specs=[pl.BlockSpec(memory_space=pl.ANY)] * len(arrays),
+        out_specs=(vmem, vmem, vmem),
+        scratch_shapes=[pltpu.VMEM(array.shape, array.dtype) for array in arrays]
+        + [
+            dma((len(arrays),)),
+            pltpu.VMEM((groups + ghosts, 3 * rows, LANES), jnp.float32),
+            pltpu.VMEM((groups + ghosts, rows, LANES), jnp.int32),
+            pltpu.VMEM((groups, faces, rows, LANES), jnp.float32),
+            pltpu.VMEM((groups, faces, rows, LANES), jnp.int32),
+            pltpu.VMEM((bins, 3, groups, LANES), jnp.float32),
+            pltpu.VMEM((ghosts, 3 * rows, LANES), jnp.float32),
+            pltpu.VMEM((groups, rows, LANES), jnp.float32),
+            pltpu.VMEM((groups, rows, LANES), jnp.bfloat16),
+            pltpu.VMEM((bins, rows, LANES), jnp.bfloat16),
+            pltpu.VMEM((bins, rows, LANES), jnp.float32),
+            pltpu.VMEM((bins, rows, LANES), jnp.float32),
+            dma((bins,)),
+            dma((bins,)),
+            dma((ghosts,)),
+            dma((ghosts,)),
+            dma((ghosts,)),
+            dma((ghosts,)),
+            dma((bins,)),
+            dma((bins,)),
+            dma((bins,)),
+            dma((bins,)),
+        ],
+        compiler_params=pltpu.CompilerParams(collective_id=0, has_side_effects=True),
+    )(*arrays)
 
 
 def solution(mesh):

time: 40 us -> 37 us (0.925)
  the two profiles are of different devices: /device:TPU:8 before, /device:TPU:4 now
where the time goes in v2:
time: 37 us; the launch traced here: 36.8 us
  Pallas kernels  33.3 us (90%)
  local copies, waits for them, and re-layouts  2.81 us (8%)
  between operations  0.65 us (2%)
    pallas_call x1, Pallas kernels, body(): pl.pallas_call(run, name='dust_step', out_shape=(jax.ShapeDtypeStruct(dus...  33.3 us
    unnamed x7, local copies, waits for them, and re-layouts  2.81 us

profile of v2, /device:TPU:4, one launch (start us, length us, event | category | flops | bytes accessed | tf_op | source)
XLA Modules:
  0.0 36.8 jit_solution(12468236474787876097)
XLA Ops:
  0.6 33.3 %dust_step.1 = (f32[16,1024]{1,0:T(8,128)}, f32[2,16,1024]{2,1,0:T(8,128)}, f32[2,1024]{1,0:T(2,128)}) custom-call(f32[16,1024]{1,0:T(8,128)} %refs_0_.1, f32[2,16,1024]{2,1,0:T(8,128)} %refs_1_.1, f32[8,128]{1,0:T(8,128)} %bitcast.5, f32[2,1024]{1,0:T(2,128)} %refs_3_.1, f32[2,8,1024]{2,1,0:T(8,128)} %refs_4_.1, f32[8,128]{1,0:T(8,128)} %bitcast.6, ...), custom_call_target="tpu_custom_call" | custom-call | tf_op jit(solution)/shard_map/dust_step/pallas_call | solution.py:358
  34.0 0.0 copy-start
  34.0 1.5 %copy.18 = f32[16,1024]{1,0:T(8,128)} copy(f32[16,1024]{1,0:T(8,128)} %get-tuple-element.6) | data formatting | bytes 131072
  35.5 0.0 copy-done
  35.5 0.0 copy-start.1
  35.5 0.7 %copy.19 = f32[2,16,1024]{2,1,0:T(8,128)} copy(f32[2,16,1024]{2,1,0:T(8,128)S(1)} %copy-done) | data formatting | bytes 262144
  36.2 0.0 copy-done.1
  36.2 0.6 %copy.20 = f32[2,1024]{1,0:T(2,128)} copy(f32[2,1024]{1,0:T(2,128)S(1)} %copy-done.1) | data formatting | bytes 16384
Async XLA Ops:
  34.0 1.5 %copy-start = (f32[2,16,1024]{2,1,0:T(8,128)S(1)}, f32[2,16,1024]{2,1,0:T(8,128)}, u32[]{:S(2)}) copy-start(f32[2,16,1024]{2,1,0:T(8,128)} %get-tuple-element.7) | copy-start | bytes 393220
  35.5 0.7 %copy-start.1 = (f32[2,1024]{1,0:T(2,128)S(1)}, f32[2,1024]{1,0:T(2,128)}, u32[]{:S(2)}) copy-start(f32[2,1024]{1,0:T(2,128)} %get-tuple-element.8) | copy-start | bytes 24580

commit v3 on v2

--- a/solution.py
+++ b/solution.py
@@ -315,6 +315,18 @@
         ghost_copy(j, rows, 3 * rows, vel_send, vel_recv).wait_send()
 
 
+def store_body(rho, vel, gas, rho_out, vel_out, gas_out, stored):
+    pairs = ((rho, rho_out), (vel, vel_out), (gas, gas_out))
+    copies = [
+        pltpu.make_async_copy(source, target, stored.at[i])
+        for i, (source, target) in enumerate(pairs)
+    ]
+    for copy in copies:
+        copy.start()
+    for copy in copies:
+        copy.wait()
+
+
 def body(
     dust_rho,
     dust_vel,
@@ -353,16 +365,13 @@
         kernel,
         redistrib,
     )
+    shapes = (dust_rho.shape, dust_vel.shape, gas_vel.shape)
     vmem = pl.BlockSpec(memory_space=pltpu.VMEM)
     dma = pltpu.SemaphoreType.DMA
-    return pl.pallas_call(
+    results = pl.pallas_call(
         run,
         name="dust_step",
-        out_shape=(
-            jax.ShapeDtypeStruct(dust_rho.shape, jnp.float32),
-            jax.ShapeDtypeStruct(dust_vel.shape, jnp.float32),
-            jax.ShapeDtypeStruct(gas_vel.shape, jnp.float32),
-        ),
+        out_shape=tuple(pltpu.VMEM(shape, jnp.float32) for shape in shapes),
         in_specs=[pl.BlockSpec(memory_space=pl.ANY)] * len(arrays),
         out_specs=(vmem, vmem, vmem),
         scratch_shapes=[pltpu.VMEM(array.shape, array.dtype) for array in arrays]
@@ -392,6 +401,15 @@
         ],
         compiler_params=pltpu.CompilerParams(collective_id=0, has_side_effects=True),
     )(*arrays)
+    return pl.pallas_call(
+        store_body,
+        name="dust_store",
+        out_shape=tuple(jax.ShapeDtypeStruct(shape, jnp.float32) for shape in shapes),
+        in_specs=[vmem] * 3,
+        out_specs=(pl.BlockSpec(memory_space=pl.ANY),) * 3,
+        scratch_shapes=[dma((3,))],
+        compiler_params=pltpu.CompilerParams(vmem_limit_bytes=1 << 20),
+    )(*results)
 
 
 def solution(mesh):

time: 37 us -> 34.2 us (0.924)
  local copies, waits for them, and re-layouts: 2.81 us -> 0 us
    unnamed x7 -> x0, local copies, waits for them, and re-layouts: 2.81 us -> none
    pallas_call x1 -> x2, Pallas kernels: 33.3 us -> 33.4 us  [the longest x1 32.7 us: body(): pl.pallas_call(run, name='dust_step', out_shape=tuple((pltpu.VMEM(shape,...]
where the time goes in v3:
time: 34.2 us; the launch traced here: 34 us
  Pallas kernels  33.4 us (98%)
  between operations  0.64 us (2%)
    pallas_call x1, Pallas kernels, body(): pl.pallas_call(run, name='dust_step', out_shape=tuple((pltpu.VMEM(shape,...  32.7 us
    pallas_call x1, Pallas kernels, body(): pl.pallas_call(store_body, name='dust_store', out_shape=tuple((jax.ShapeD...  0.71 us

profile of v3, /device:TPU:4, one launch (start us, length us, event | category | flops | bytes accessed | tf_op | source)
XLA Modules:
  0.0 34.0 jit_solution(4354449174862471409)
XLA Ops:
  0.6 32.7 %dust_step.1 = (f32[16,1024]{1,0:T(8,128)S(1)}, f32[2,16,1024]{2,1,0:T(8,128)S(1)}, f32[2,1024]{1,0:T(2,128)S(1)}) custom-call(f32[16,1024]{1,0:T(8,128)} %refs_0_.1, f32[2,16,1024]{2,1,0:T(8,128)} %refs_1_.1, f32[8,128]{1,0:T(8,128)} %bitcast.5, f32[2,1024]{1,0:T(2,128)} %refs_3_.1, f32[2,8,1024]{2,1,0:T(8,128)} %refs_4_.1, f32[8,128]{1,0:T(8,128)} %bitcast.6, ...), custom_call_target="tpu_custom_call" | custom-call | tf_op jit(solution)/shard_map/dust_step/pallas_call | solution.py:371
  33.3 0.7 %dust_store.1 = (f32[16,1024]{1,0:T(8,128)}, f32[2,16,1024]{2,1,0:T(8,128)}, f32[2,1024]{1,0:T(2,128)}) custom-call(f32[16,1024]{1,0:T(8,128)S(1)} %get-tuple-element.6.rho, f32[2,16,1024]{2,1,0:T(8,128)S(1)} %get-tuple-element.7.vel, f32[2,1024]{1,0:T(2,128)S(1)} %get-tuple-element.8.gas), custom_call_target="tpu_custom_call" | custom-call | tf_op jit(solution)/shard_map/dust_store/pallas_call | solution.py:404

commit v4 on v3

--- a/solution.py
+++ b/solution.py
@@ -62,8 +62,14 @@
         coded,
         picked,
         picked_vel,
+        partial,
         sums,
-        ghost_out,
+        gas_held,
+        fixed,
+        share_held,
+        ghost_rho,
+        ghost_vel,
+        ghost_in,
         moved,
         rounded,
         mixed,
@@ -124,36 +130,46 @@
         gas_rho = gas_rho_ref[c : c + 1, :]
         coupling = drag * gas_rho
         weight = density / gas_rho * (coupling / (1.0 + coupling))
-        sums[me, 0, c : c + 1, :] = jnp.sum(weight, axis=0, keepdims=True)
-        sums[me, 1, c : c + 1, :] = jnp.sum(weight * vel_ref[0, :, cells], axis=0, keepdims=True)
-        sums[me, 2, c : c + 1, :] = jnp.sum(weight * vel_ref[1, :, cells], axis=0, keepdims=True)
-
-    def choose(first_row, last_row):
+        partial[0, c : c + 1, :] = jnp.sum(weight, axis=0, keepdims=True)
+        partial[1, c : c + 1, :] = jnp.sum(weight * vel_ref[0, :, cells], axis=0, keepdims=True)
+        partial[2, c : c + 1, :] = jnp.sum(weight * vel_ref[1, :, cells], axis=0, keepdims=True)
+    sums[me] = partial[...].astype(jnp.bfloat16)
+
+    def choose(first_row, target):
         for j in range(len(OFFSETS)):
             index = spread(send_ref[j : j + 1, :])
             safe = jnp.maximum(index, 0)
             lanes = safe & (LANES - 1)
             block = safe >> 7
-            for r in range(first_row, last_row, SUB):
+            parts = []
+            for r in range(first_row, first_row + target.shape[1], SUB):
                 value = lane_take(ext[0, r : r + SUB, :], lanes)
                 for s in range(1, groups):
                     value = jnp.where(
                         block == s, lane_take(ext[s, r : r + SUB, :], lanes), value
                     )
-                ghost_out[j, r : r + SUB, :] = jnp.where(index >= 0, value, 0.0)
-
-    def ghost_copy(j, first_row, last_row, send_sem, recv_sem):
+                parts.append(jnp.where(index >= 0, value, 0.0))
+            target[j] = jnp.concatenate(parts, axis=0).astype(target.dtype)
+
+    def ghost_copy(j, source, target, send_sem, recv_sem):
         return pltpu.make_async_remote_copy(
-            src_ref=ghost_out.at[j, first_row:last_row],
-            dst_ref=ext.at[groups + j, first_row:last_row],
+            src_ref=source,
+            dst_ref=target,
             send_sem=send_sem.at[j],
             recv_sem=recv_sem.at[j],
             device_id={"dom": lax.rem(dom + OFFSETS[j] + doms, doms)},
             device_id_type=MESH,
         )
 
+    def rho_copy(j):
+        target = ext.at[groups + j, 0:rows]
+        return ghost_copy(j, ghost_rho.at[j], target, rho_send, rho_recv)
+
+    def vel_copy(j):
+        return ghost_copy(j, ghost_vel.at[j], ghost_in.at[j], vel_send, vel_recv)
+
     loads[9].wait()
-    choose(0, rows)
+    choose(0, ghost_rho)
     pl.semaphore_wait(barrier, bins - 1 + len(OFFSETS))
 
     def peer_copy(step, source, target, send_sem, recv_sem):
@@ -170,10 +186,20 @@
         sender = lax.rem(me + bins - step, bins)
         peer_copy(step, source, buffer.at[sender], send_sem, recv_sem).wait_recv()
 
-    for step in range(1, bins):
+    order = [(bins // 2 + turn) % bins for turn in (0, 1, 7, 3, 2, 5, 6, 4)]
+    for step in order[:-1]:
         peer_copy(step, sums.at[me], sums.at[me], sum_send, sum_recv).start()
     for j in range(len(OFFSETS)):
-        ghost_copy(j, 0, rows, rho_send, rho_recv).start()
+        rho_copy(j).start()
+    loads[3].wait()
+    for c in range(groups):
+        cells = slice(c * LANES, (c + 1) * LANES)
+        coupling = drag * gas_rho_ref[c : c + 1, :]
+        inverse = 1.0 / (1.0 + coupling)
+        share_held[c] = coupling / (1.0 + coupling)
+        for component in range(2):
+            fixed[component, c] = vel_ref[component, :, cells] * inverse
+            gas_held[component, c : c + 1, :] = gas_vel_ref[component : component + 1, cells]
 
     def pick(first_block, last_block, source, target, c, faces):
         cells = pl.ds(pl.multiple_of(c * LANES, LANES), LANES)
@@ -204,42 +230,39 @@
     loads[8].wait()
     pick_all(0, groups, ext, picked)
     for j in range(len(OFFSETS)):
-        ghost_copy(j, 0, rows, rho_send, rho_recv).wait_recv()
+        rho_copy(j).wait_recv()
     pick_all(groups, total_blocks, ext, picked)
-    for i in (3, 4, 5, 6, 10, 11):
+    for i in (4, 5, 6, 10, 11):
         loads[i].wait()
 
     for step in range(1, bins):
         peer_arrived(step, sums.at[me], sums, sum_send, sum_recv)
-    totals = sums[0]
+    totals = sums[0].astype(jnp.float32)
     for b in range(1, bins):
-        totals = totals + sums[b]
-
+        totals = totals + sums[b].astype(jnp.float32)
+    gas_held[...] = (gas_held[...] + totals[1:]) / (1.0 + totals[0:1])
     for c in range(groups):
         cells = slice(c * LANES, (c + 1) * LANES)
-        scale = 1.0 + totals[0, c : c + 1, :]
-        coupling = drag * gas_rho_ref[c : c + 1, :]
+        share = share_held[c]
         both = []
         for component in range(2):
-            gas = (
-                gas_vel_ref[component : component + 1, cells]
-                + totals[component + 1, c : c + 1, :]
-            ) / scale
+            gas = gas_held[component, c : c + 1, :]
             gas_out[component : component + 1, cells] = gas
-            dust = (vel_ref[component, :, cells] + coupling * gas) / (1.0 + coupling)
+            dust = fixed[component, c] + share * gas
             vel_out[component, :, cells] = dust
             ext[c, (component + 1) * rows : (component + 2) * rows, :] = dust
             both.append(dust)
         coded[c] = join(both[0], both[1])
 
-    choose(rows, 3 * rows)
+    choose(rows, ghost_vel)
     for j in range(len(OFFSETS)):
-        ghost_copy(j, rows, 3 * rows, vel_send, vel_recv).start()
+        vel_copy(j).start()
     pick_all(0, groups, coded, picked_vel)
     for j in range(len(OFFSETS)):
-        ghost_copy(j, rows, 3 * rows, vel_send, vel_recv).wait_recv()
+        vel_copy(j).wait_recv()
         coded[groups + j] = join(
-            ext[groups + j, rows : 2 * rows, :], ext[groups + j, 2 * rows : 3 * rows, :]
+            ghost_in[j, 0:rows].astype(jnp.float32),
+            ghost_in[j, rows : 2 * rows].astype(jnp.float32),
         )
 
     def advect(c):
@@ -279,7 +302,6 @@
             moved[c, first, :] = density - inverse * total
         rounded[c] = moved[c].astype(jnp.bfloat16)
 
-    order = [(bins // 2 + turn) % bins for turn in (0, 1, 7, 3, 2, 5, 6, 4)]
     for first in range(0, bins, UNROLL):
         for step in order[first : first + UNROLL]:
             advect(lax.rem(me + step, bins))
@@ -295,15 +317,16 @@
     rate = coag_ref[pl.ds(me, 1), :]
     loss = (rate * columns.astype(jnp.float32) * collide).astype(jnp.bfloat16)
     gain = jnp.dot(redis_ref[...], loss, preferred_element_type=jnp.float32)
-    delta[...] = (gain - loss.astype(jnp.float32)).reshape(bins, rows, LANES)
-    for step in range(1, bins):
+    change = gain - loss.astype(jnp.float32)
+    delta[...] = change.astype(jnp.bfloat16).reshape(bins, rows, LANES)
+    for step in order[:-1]:
         peer = lax.rem(me + step, bins)
         peer_copy(step, delta.at[peer], back.at[me], back_send, back_recv).start()
     back[me] = delta[me]
     for step in range(1, bins):
         peer_arrived(step, delta.at[0], back, back_send, back_recv)
     for c in range(groups):
-        rho_out[:, c * LANES : (c + 1) * LANES] = moved[c] + back[c]
+        rho_out[:, c * LANES : (c + 1) * LANES] = moved[c] + back[c].astype(jnp.float32)
 
     for step in range(1, bins):
         peer = lax.rem(me + step, bins)
@@ -311,8 +334,8 @@
         peer_copy(step, rounded.at[peer], mixed.at[me], mix_send, mix_recv).wait_send()
         peer_copy(step, delta.at[peer], back.at[me], back_send, back_recv).wait_send()
     for j in range(len(OFFSETS)):
-        ghost_copy(j, 0, rows, rho_send, rho_recv).wait_send()
-        ghost_copy(j, rows, 3 * rows, vel_send, vel_recv).wait_send()
+        rho_copy(j).wait_send()
+        vel_copy(j).wait_send()
 
 
 def store_body(rho, vel, gas, rho_out, vel_out, gas_out, stored):
@@ -381,13 +404,19 @@
             pltpu.VMEM((groups + ghosts, rows, LANES), jnp.int32),
             pltpu.VMEM((groups, faces, rows, LANES), jnp.float32),
             pltpu.VMEM((groups, faces, rows, LANES), jnp.int32),
-            pltpu.VMEM((bins, 3, groups, LANES), jnp.float32),
-            pltpu.VMEM((ghosts, 3 * rows, LANES), jnp.float32),
+            pltpu.VMEM((3, groups, LANES), jnp.float32),
+            pltpu.VMEM((bins, 3, groups, LANES), jnp.bfloat16),
+            pltpu.VMEM((2, groups, LANES), jnp.float32),
+            pltpu.VMEM((2, groups, rows, LANES), jnp.float32),
+            pltpu.VMEM((groups, rows, LANES), jnp.float32),
+            pltpu.VMEM((ghosts, rows, LANES), jnp.float32),
+            pltpu.VMEM((ghosts, 2 * rows, LANES), jnp.bfloat16),
+            pltpu.VMEM((ghosts, 2 * rows, LANES), jnp.bfloat16),
             pltpu.VMEM((groups, rows, LANES), jnp.float32),
             pltpu.VMEM((groups, rows, LANES), jnp.bfloat16),
             pltpu.VMEM((bins, rows, LANES), jnp.bfloat16),
-            pltpu.VMEM((bins, rows, LANES), jnp.float32),
-            pltpu.VMEM((bins, rows, LANES), jnp.float32),
+            pltpu.VMEM((bins, rows, LANES), jnp.bfloat16),
+            pltpu.VMEM((bins, rows, LANES), jnp.bfloat16),
             dma((bins,)),
             dma((bins,)),
             dma((ghosts,)),

time: 34.2 us -> 33.3 us (0.974)
  Pallas kernels: 33.4 us -> 32.6 us
    pallas_call x1, Pallas kernels: 32.7 us -> 31.9 us  [body(): pl.pallas_call(run, name='dust_step', out_shape=tuple((pltpu.VMEM(shape,...]
where the time goes in v4:
time: 33.3 us; the launch traced here: 33.2 us
  Pallas kernels  32.6 us (98%)
  between operations  0.64 us (2%)
    pallas_call x1, Pallas kernels, body(): pl.pallas_call(run, name='dust_step', out_shape=tuple((pltpu.VMEM(shape,...  31.9 us
    pallas_call x1, Pallas kernels, body(): pl.pallas_call(store_body, name='dust_store', out_shape=tuple((jax.ShapeD...  0.71 us

profile of v4, /device:TPU:4, one launch (start us, length us, event | category | flops | bytes accessed | tf_op | source)
XLA Modules:
  0.0 33.2 jit_solution(16288657668930603831)
XLA Ops:
  0.6 31.9 %dust_step.1 = (f32[16,1024]{1,0:T(8,128)S(1)}, f32[2,16,1024]{2,1,0:T(8,128)S(1)}, f32[2,1024]{1,0:T(2,128)S(1)}) custom-call(f32[16,1024]{1,0:T(8,128)} %refs_0_.1, f32[2,16,1024]{2,1,0:T(8,128)} %refs_1_.1, f32[8,128]{1,0:T(8,128)} %bitcast.5, f32[2,1024]{1,0:T(2,128)} %refs_3_.1, f32[2,8,1024]{2,1,0:T(8,128)} %refs_4_.1, f32[8,128]{1,0:T(8,128)} %bitcast.6, ...), custom_call_target="tpu_custom_call" | custom-call | tf_op jit(solution)/shard_map/dust_step/pallas_call | solution.py:394
  32.5 0.7 %dust_store.1 = (f32[16,1024]{1,0:T(8,128)}, f32[2,16,1024]{2,1,0:T(8,128)}, f32[2,1024]{1,0:T(2,128)}) custom-call(f32[16,1024]{1,0:T(8,128)S(1)} %get-tuple-element.6.rho, f32[2,16,1024]{2,1,0:T(8,128)S(1)} %get-tuple-element.7.vel, f32[2,1024]{1,0:T(2,128)S(1)} %get-tuple-element.8.gas), custom_call_target="tpu_custom_call" | custom-call | tf_op jit(solution)/shard_map/dust_store/pallas_call | solution.py:433

commit v5 on v4

--- a/solution.py
+++ b/solution.py
@@ -62,8 +62,11 @@
         coded,
         picked,
         picked_vel,
+        after,
         partial,
         sums,
+        ghost_partial,
+        ghost_sums,
         gas_held,
         fixed,
         share_held,
@@ -77,6 +80,8 @@
         back,
         sum_send,
         sum_recv,
+        add_send,
+        add_recv,
         rho_send,
         rho_recv,
         vel_send,
@@ -109,9 +114,9 @@
     loads = [
         pltpu.make_async_copy(held[i], inputs[i], loaded.at[i]) for i in range(len(inputs))
     ]
-    for i in (0, 2, 7, 9, 1, 8, 3, 4, 5, 6, 10, 11):
+    for i in (0, 2, 7, 1, 3, 9, 8, 4, 5, 6, 10, 11):
         loads[i].start()
-    for i in (0, 2, 7, 1):
+    for i in (0, 2, 7, 1, 3):
         loads[i].wait()
 
     diagonal = lax.broadcasted_iota(jnp.int32, (rows, rows), 0) == lax.broadcasted_iota(
@@ -128,6 +133,9 @@
         density = rho_ref[:, cells]
         ext[c, 0:rows, :] = density
         gas_rho = gas_rho_ref[c : c + 1, :]
+        ext[c, rows : rows + SUB, :] = jnp.zeros((SUB, LANES), jnp.float32)
+        ext[c, rows : rows + 1, :] = gas_rho
+        ext[c, rows + 1 : rows + 3, :] = gas_vel_ref[:, cells]
         coupling = drag * gas_rho
         weight = density / gas_rho * (coupling / (1.0 + coupling))
         partial[0, c : c + 1, :] = jnp.sum(weight, axis=0, keepdims=True)
@@ -135,19 +143,17 @@
         partial[2, c : c + 1, :] = jnp.sum(weight * vel_ref[1, :, cells], axis=0, keepdims=True)
     sums[me] = partial[...].astype(jnp.bfloat16)
 
-    def choose(first_row, target):
+    def choose(fetch, target):
         for j in range(len(OFFSETS)):
             index = spread(send_ref[j : j + 1, :])
             safe = jnp.maximum(index, 0)
             lanes = safe & (LANES - 1)
             block = safe >> 7
             parts = []
-            for r in range(first_row, first_row + target.shape[1], SUB):
-                value = lane_take(ext[0, r : r + SUB, :], lanes)
+            for i in range(target.shape[1] // SUB):
+                value = lane_take(fetch(0, i), lanes)
                 for s in range(1, groups):
-                    value = jnp.where(
-                        block == s, lane_take(ext[s, r : r + SUB, :], lanes), value
-                    )
+                    value = jnp.where(block == s, lane_take(fetch(s, i), lanes), value)
                 parts.append(jnp.where(index >= 0, value, 0.0))
             target[j] = jnp.concatenate(parts, axis=0).astype(target.dtype)
 
@@ -162,14 +168,19 @@
         )
 
     def rho_copy(j):
-        target = ext.at[groups + j, 0:rows]
-        return ghost_copy(j, ghost_rho.at[j], target, rho_send, rho_recv)
+        return ghost_copy(j, ghost_rho.at[j], ext.at[groups + j], rho_send, rho_recv)
 
     def vel_copy(j):
         return ghost_copy(j, ghost_vel.at[j], ghost_in.at[j], vel_send, vel_recv)
 
     loads[9].wait()
-    choose(0, ghost_rho)
+    choose(lambda s, i: ext[s, i * SUB : (i + 1) * SUB, :], ghost_rho)
+
+    def own_vel(s, i):
+        row = i % halves * SUB
+        return vel_ref[i // halves, row : row + SUB, s * LANES : (s + 1) * LANES]
+
+    choose(own_vel, ghost_vel)
     pl.semaphore_wait(barrier, bins - 1 + len(OFFSETS))
 
     def peer_copy(step, source, target, send_sem, recv_sem):
@@ -187,11 +198,11 @@
         peer_copy(step, source, buffer.at[sender], send_sem, recv_sem).wait_recv()
 
     order = [(bins // 2 + turn) % bins for turn in (0, 1, 7, 3, 2, 5, 6, 4)]
+    for j in range(len(OFFSETS)):
+        rho_copy(j).start()
+        vel_copy(j).start()
     for step in order[:-1]:
         peer_copy(step, sums.at[me], sums.at[me], sum_send, sum_recv).start()
-    for j in range(len(OFFSETS)):
-        rho_copy(j).start()
-    loads[3].wait()
     for c in range(groups):
         cells = slice(c * LANES, (c + 1) * LANES)
         coupling = drag * gas_rho_ref[c : c + 1, :]
@@ -231,6 +242,25 @@
     pick_all(0, groups, ext, picked)
     for j in range(len(OFFSETS)):
         rho_copy(j).wait_recv()
+        vel_copy(j).wait_recv()
+    ghost_partial[...] = jnp.zeros_like(ghost_partial)
+    for j in range(len(OFFSETS)):
+        gas_rho = ext[groups + j, rows : rows + 1, :]
+        gas_rho = jnp.where(gas_rho > 0.0, gas_rho, 1.0)
+        coupling = drag * gas_rho
+        inverse = 1.0 / (1.0 + coupling)
+        share = coupling / (1.0 + coupling)
+        share_held[groups + j] = share
+        weight = ext[groups + j, 0:rows, :] / gas_rho * share
+        ghost_partial[j : j + 1, :] = jnp.sum(weight, axis=0, keepdims=True)
+        for component in range(2):
+            vel = ghost_in[j, component * rows : (component + 1) * rows].astype(jnp.float32)
+            fixed[component, groups + j] = vel * inverse
+            row = (component + 1) * len(OFFSETS) + j
+            ghost_partial[row : row + 1, :] = jnp.sum(weight * vel, axis=0, keepdims=True)
+    ghost_sums[me] = ghost_partial[...].astype(jnp.bfloat16)
+    for step in order[:-1]:
+        peer_copy(step, ghost_sums.at[me], ghost_sums.at[me], add_send, add_recv).start()
     pick_all(groups, total_blocks, ext, picked)
     for i in (4, 5, 6, 10, 11):
         loads[i].wait()
@@ -250,20 +280,24 @@
             gas_out[component : component + 1, cells] = gas
             dust = fixed[component, c] + share * gas
             vel_out[component, :, cells] = dust
-            ext[c, (component + 1) * rows : (component + 2) * rows, :] = dust
+            after[c, component * rows : (component + 1) * rows, :] = dust
             both.append(dust)
         coded[c] = join(both[0], both[1])
 
-    choose(rows, ghost_vel)
+    pick_all(0, groups, coded, picked_vel)
+    for step in range(1, bins):
+        peer_arrived(step, ghost_sums.at[me], ghost_sums, add_send, add_recv)
+    totals = ghost_sums[0].astype(jnp.float32)
+    for b in range(1, bins):
+        totals = totals + ghost_sums[b].astype(jnp.float32)
     for j in range(len(OFFSETS)):
-        vel_copy(j).start()
-    pick_all(0, groups, coded, picked_vel)
-    for j in range(len(OFFSETS)):
-        vel_copy(j).wait_recv()
-        coded[groups + j] = join(
-            ghost_in[j, 0:rows].astype(jnp.float32),
-            ghost_in[j, rows : 2 * rows].astype(jnp.float32),
-        )
+        both = []
+        for component in range(2):
+            row = (component + 1) * len(OFFSETS) + j
+            given = ext[groups + j, rows + 1 + component : rows + 2 + component, :]
+            gas = (given + totals[row : row + 1, :]) / (1.0 + totals[j : j + 1, :])
+            both.append(fixed[component, groups + j] + share_held[groups + j] * gas)
+        coded[groups + j] = join(both[0], both[1])
 
     def advect(c):
         pick(groups, total_blocks, coded, picked_vel, c, range(face_count))
@@ -276,10 +310,9 @@
         for h in range(halves):
             first = slice(h * SUB, (h + 1) * SUB)
             second = slice(rows + h * SUB, rows + (h + 1) * SUB)
-            third = slice(2 * rows + h * SUB, 2 * rows + (h + 1) * SUB)
             density = ext[c, first, :]
-            vel_x = ext[c, second, :] - MIDDLE / STEPS
-            vel_y = ext[c, third, :] - MIDDLE / STEPS
+            vel_x = after[c, first, :] - MIDDLE / STEPS
+            vel_y = after[c, second, :] - MIDDLE / STEPS
             mean = jnp.where(valid[0], picked[c, 0, first, :], 0.0)
             for k in range(1, face_count):
                 mean = mean + jnp.where(valid[k], picked[c, k, first, :], 0.0)
@@ -331,6 +364,7 @@
     for step in range(1, bins):
         peer = lax.rem(me + step, bins)
         peer_copy(step, sums.at[me], sums.at[me], sum_send, sum_recv).wait_send()
+        peer_copy(step, ghost_sums.at[me], ghost_sums.at[me], add_send, add_recv).wait_send()
         peer_copy(step, rounded.at[peer], mixed.at[me], mix_send, mix_recv).wait_send()
         peer_copy(step, delta.at[peer], back.at[me], back_send, back_recv).wait_send()
     for j in range(len(OFFSETS)):
@@ -400,16 +434,19 @@
         scratch_shapes=[pltpu.VMEM(array.shape, array.dtype) for array in arrays]
         + [
             dma((len(arrays),)),
-            pltpu.VMEM((groups + ghosts, 3 * rows, LANES), jnp.float32),
+            pltpu.VMEM((groups + ghosts, rows + SUB, LANES), jnp.float32),
             pltpu.VMEM((groups + ghosts, rows, LANES), jnp.int32),
             pltpu.VMEM((groups, faces, rows, LANES), jnp.float32),
             pltpu.VMEM((groups, faces, rows, LANES), jnp.int32),
+            pltpu.VMEM((groups, 2 * rows, LANES), jnp.float32),
             pltpu.VMEM((3, groups, LANES), jnp.float32),
             pltpu.VMEM((bins, 3, groups, LANES), jnp.bfloat16),
+            pltpu.VMEM((4 * ghosts, LANES), jnp.float32),
+            pltpu.VMEM((bins, 4 * ghosts, LANES), jnp.bfloat16),
             pltpu.VMEM((2, groups, LANES), jnp.float32),
-            pltpu.VMEM((2, groups, rows, LANES), jnp.float32),
-            pltpu.VMEM((groups, rows, LANES), jnp.float32),
-            pltpu.VMEM((ghosts, rows, LANES), jnp.float32),
+            pltpu.VMEM((2, groups + ghosts, rows, LANES), jnp.float32),
+            pltpu.VMEM((groups + ghosts, rows, LANES), jnp.float32),
+            pltpu.VMEM((ghosts, rows + SUB, LANES), jnp.float32),
             pltpu.VMEM((ghosts, 2 * rows, LANES), jnp.bfloat16),
             pltpu.VMEM((ghosts, 2 * rows, LANES), jnp.bfloat16),
             pltpu.VMEM((groups, rows, LANES), jnp.float32),
@@ -417,6 +454,8 @@
             pltpu.VMEM((bins, rows, LANES), jnp.bfloat16),
             pltpu.VMEM((bins, rows, LANES), jnp.bfloat16),
             pltpu.VMEM((bins, rows, LANES), jnp.bfloat16),
+            dma((bins,)),
+            dma((bins,)),
             dma((bins,)),
             dma((bins,)),
             dma((ghosts,)),

time: 33.3 us -> 33.7 us (1.012)
  the two profiles are of different devices: /device:TPU:4 before, /device:TPU:8 now
where the time goes in v5:
time: 33.7 us; the launch traced here: 33.5 us
  Pallas kernels  32.9 us (98%)
  between operations  0.64 us (2%)
    pallas_call x1, Pallas kernels, body(): pl.pallas_call(run, name='dust_step', out_shape=tuple((pltpu.VMEM(shape,...  32.2 us
    pallas_call x1, Pallas kernels, body(): pl.pallas_call(store_body, name='dust_store', out_shape=tuple((jax.ShapeD...  0.71 us

profile of v5, /device:TPU:8, one launch (start us, length us, event | category | flops | bytes accessed | tf_op | source)
XLA Modules:
  0.0 33.5 jit_solution(3829454116919555494)
XLA Ops:
  0.6 32.2 %dust_step.1 = (f32[16,1024]{1,0:T(8,128)S(1)}, f32[2,16,1024]{2,1,0:T(8,128)S(1)}, f32[2,1024]{1,0:T(2,128)S(1)}) custom-call(f32[16,1024]{1,0:T(8,128)} %refs_0_.1, f32[2,16,1024]{2,1,0:T(8,128)} %refs_1_.1, f32[8,128]{1,0:T(8,128)} %bitcast.5, f32[2,1024]{1,0:T(2,128)} %refs_3_.1, f32[2,8,1024]{2,1,0:T(8,128)} %refs_4_.1, f32[8,128]{1,0:T(8,128)} %bitcast.6, ...), custom_call_target="tpu_custom_call" | custom-call | tf_op jit(solution)/shard_map/dust_step/pallas_call | solution.py:428
  32.8 0.7 %dust_store.1 = (f32[16,1024]{1,0:T(8,128)}, f32[2,16,1024]{2,1,0:T(8,128)}, f32[2,1024]{1,0:T(2,128)}) custom-call(f32[16,1024]{1,0:T(8,128)S(1)} %get-tuple-element.6.rho, f32[2,16,1024]{2,1,0:T(8,128)S(1)} %get-tuple-element.7.vel, f32[2,1024]{1,0:T(2,128)S(1)} %get-tuple-element.8.gas), custom_call_target="tpu_custom_call" | custom-call | tf_op jit(solution)/shard_map/dust_store/pallas_call | solution.py:472

commit v6 on v4

--- a/solution.py
+++ b/solution.py
@@ -62,6 +62,9 @@
         coded,
         picked,
         picked_vel,
+        outward,
+        inward,
+        base,
         partial,
         sums,
         gas_held,
@@ -235,6 +238,28 @@
     for i in (4, 5, 6, 10, 11):
         loads[i].wait()
 
+    def limit(c, carry):
+        cells = pl.ds(pl.multiple_of(c * LANES, LANES), LANES)
+        valid = [spread(faces_ref[k : k + 1, cells]) >= 0 for k in range(face_count)]
+        count = valid[0].astype(jnp.float32)
+        for k in range(1, face_count):
+            count = count + valid[k].astype(jnp.float32)
+        for h in range(halves):
+            first = slice(h * SUB, (h + 1) * SUB)
+            density = ext[c, first, :]
+            mean = jnp.where(valid[0], picked[c, 0, first, :], 0.0)
+            for k in range(1, face_count):
+                mean = mean + jnp.where(valid[k], picked[c, k, first, :], 0.0)
+            slope = density - mean / count
+            for k in range(face_count):
+                other = picked[c, k, first, :]
+                limited = 0.5 * minmod(other - density, slope)
+                outward[c, k, first, :] = jnp.where(valid[k], density + limited, 0.0)
+                inward[c, k, first, :] = jnp.where(valid[k], other - limited, 0.0)
+        return carry
+
+    lax.fori_loop(0, groups, limit, 0)
+
     for step in range(1, bins):
         peer_arrived(step, sums.at[me], sums, sum_send, sum_recv)
     totals = sums[0].astype(jnp.float32)
@@ -258,6 +283,21 @@
     for j in range(len(OFFSETS)):
         vel_copy(j).start()
     pick_all(0, groups, coded, picked_vel)
+
+    def prepare(c, carry):
+        cells = pl.ds(pl.multiple_of(c * LANES, LANES), LANES)
+        for h in range(halves):
+            first = slice(h * SUB, (h + 1) * SUB)
+            vel_x = ext[c, rows + h * SUB : rows + (h + 1) * SUB, :] - MIDDLE / STEPS
+            vel_y = ext[c, 2 * rows + h * SUB : 2 * rows + (h + 1) * SUB, :] - MIDDLE / STEPS
+            for k in range(face_count):
+                base[c, k, first, :] = 0.5 * (
+                    vel_x * spread(normals_ref[0, k : k + 1, cells])
+                    + vel_y * spread(normals_ref[1, k : k + 1, cells])
+                )
+        return carry
+
+    lax.fori_loop(0, groups, prepare, 0)
     for j in range(len(OFFSETS)):
         vel_copy(j).wait_recv()
         coded[groups + j] = join(
@@ -268,38 +308,24 @@
     def advect(c):
         pick(groups, total_blocks, coded, picked_vel, c, range(face_count))
         cells = pl.ds(pl.multiple_of(c * LANES, LANES), LANES)
-        valid = [spread(faces_ref[k : k + 1, cells]) >= 0 for k in range(face_count)]
-        count = valid[0].astype(jnp.float32)
-        for k in range(1, face_count):
-            count = count + valid[k].astype(jnp.float32)
-        inverse = spread(inv_ref[pl.ds(c, 1), :])
+        volume = spread(inv_ref[pl.ds(c, 1), :])
+        total = [jnp.zeros((SUB, LANES), jnp.float32) for h in range(halves)]
+        for k in range(face_count):
+            normal_x = spread(normals_ref[0, k : k + 1, cells]) * (0.5 / STEPS)
+            normal_y = spread(normals_ref[1, k : k + 1, cells]) * (0.5 / STEPS)
+            for h in range(halves):
+                first = slice(h * SUB, (h + 1) * SUB)
+                pair = picked_vel[c, k, first, :]
+                other_x = lax.shift_right_logical(pair, 16).astype(jnp.float32)
+                other_y = (pair & 65535).astype(jnp.float32)
+                speed = base[c, k, first, :] + (other_x * normal_x + other_y * normal_y)
+                total[h] = total[h] + (
+                    jnp.maximum(speed, 0.0) * outward[c, k, first, :]
+                    + jnp.minimum(speed, 0.0) * inward[c, k, first, :]
+                )
         for h in range(halves):
             first = slice(h * SUB, (h + 1) * SUB)
-            second = slice(rows + h * SUB, rows + (h + 1) * SUB)
-            third = slice(2 * rows + h * SUB, 2 * rows + (h + 1) * SUB)
-            density = ext[c, first, :]
-            vel_x = ext[c, second, :] - MIDDLE / STEPS
-            vel_y = ext[c, third, :] - MIDDLE / STEPS
-            mean = jnp.where(valid[0], picked[c, 0, first, :], 0.0)
-            for k in range(1, face_count):
-                mean = mean + jnp.where(valid[k], picked[c, k, first, :], 0.0)
-            slope = density - mean / count
-            total = jnp.zeros((SUB, LANES), jnp.float32)
-            for k in range(face_count):
-                other = picked[c, k, first, :]
-                pair = picked_vel[c, k, first, :]
-                other_x = lax.shift_right_logical(pair, 16).astype(jnp.float32) * (1.0 / STEPS)
-                other_y = (pair & 65535).astype(jnp.float32) * (1.0 / STEPS)
-                speed = 0.5 * (
-                    (vel_x + other_x) * spread(normals_ref[0, k : k + 1, cells])
-                    + (vel_y + other_y) * spread(normals_ref[1, k : k + 1, cells])
-                )
-                limited = 0.5 * minmod(other - density, slope)
-                flux = jnp.maximum(speed, 0.0) * (density + limited) + jnp.minimum(speed, 0.0) * (
-                    other - limited
-                )
-                total = total + jnp.where(valid[k], flux, 0.0)
-            moved[c, first, :] = density - inverse * total
+            moved[c, first, :] = ext[c, first, :] - volume * total[h]
         rounded[c] = moved[c].astype(jnp.bfloat16)
 
     for first in range(0, bins, UNROLL):
@@ -404,6 +430,9 @@
             pltpu.VMEM((groups + ghosts, rows, LANES), jnp.int32),
             pltpu.VMEM((groups, faces, rows, LANES), jnp.float32),
             pltpu.VMEM((groups, faces, rows, LANES), jnp.int32),
+            pltpu.VMEM((groups, faces, rows, LANES), jnp.float32),
+            pltpu.VMEM((groups, faces, rows, LANES), jnp.float32),
+            pltpu.VMEM((groups, faces, rows, LANES), jnp.float32),
             pltpu.VMEM((3, groups, LANES), jnp.float32),
             pltpu.VMEM((bins, 3, groups, LANES), jnp.bfloat16),
             pltpu.VMEM((2, groups, LANES), jnp.float32),

time: 33.3 us -> 33.6 us (level)
  the two profiles are of different devices: /device:TPU:4 before, /device:TPU:8 now
where the time goes in v6:
time: 33.6 us; the launch traced here: 33.4 us
  Pallas kernels  32.8 us (98%)
  between operations  0.64 us (2%)
    pallas_call x1, Pallas kernels, body(): pl.pallas_call(run, name='dust_step', out_shape=tuple((pltpu.VMEM(shape,...  32.1 us
    pallas_call x1, Pallas kernels, body(): pl.pallas_call(store_body, name='dust_store', out_shape=tuple((jax.ShapeD...  0.71 us

profile of v6, /device:TPU:8, one launch (start us, length us, event | category | flops | bytes accessed | tf_op | source)
XLA Modules:
  0.0 33.4 jit_solution(2618416137481057441)
XLA Ops:
  0.6 32.1 %dust_step.1 = (f32[16,1024]{1,0:T(8,128)S(1)}, f32[2,16,1024]{2,1,0:T(8,128)S(1)}, f32[2,1024]{1,0:T(2,128)S(1)}) custom-call(f32[16,1024]{1,0:T(8,128)} %refs_0_.1, f32[2,16,1024]{2,1,0:T(8,128)} %refs_1_.1, f32[8,128]{1,0:T(8,128)} %bitcast.5, f32[2,1024]{1,0:T(2,128)} %refs_3_.1, f32[2,8,1024]{2,1,0:T(8,128)} %refs_4_.1, f32[8,128]{1,0:T(8,128)} %bitcast.6, ...), custom_call_target="tpu_custom_call" | custom-call | tf_op jit(solution)/shard_map/dust_step/pallas_call | solution.py:420
  32.7 0.7 %dust_store.1 = (f32[16,1024]{1,0:T(8,128)}, f32[2,16,1024]{2,1,0:T(8,128)}, f32[2,1024]{1,0:T(2,128)}) custom-call(f32[16,1024]{1,0:T(8,128)S(1)} %get-tuple-element.6.rho, f32[2,16,1024]{2,1,0:T(8,128)S(1)} %get-tuple-element.7.vel, f32[2,1024]{1,0:T(2,128)S(1)} %get-tuple-element.8.gas), custom_call_target="tpu_custom_call" | custom-call | tf_op jit(solution)/shard_map/dust_store/pallas_call | solution.py:462

commit v7 on v4

--- a/solution.py
+++ b/solution.py
@@ -187,8 +187,13 @@
         peer_copy(step, source, buffer.at[sender], send_sem, recv_sem).wait_recv()
 
     order = [(bins // 2 + turn) % bins for turn in (0, 1, 7, 3, 2, 5, 6, 4)]
+    odd = lax.rem(dom, 2)
+
+    def turned(step):
+        return step + odd * (bins - 2 * step)
+
     for step in order[:-1]:
-        peer_copy(step, sums.at[me], sums.at[me], sum_send, sum_recv).start()
+        peer_copy(turned(step), sums.at[me], sums.at[me], sum_send, sum_recv).start()
     for j in range(len(OFFSETS)):
         rho_copy(j).start()
     loads[3].wait()
@@ -304,11 +309,11 @@
 
     for first in range(0, bins, UNROLL):
         for step in order[first : first + UNROLL]:
-            advect(lax.rem(me + step, bins))
+            advect(lax.rem(me + turned(step), bins))
         for step in order[first : first + UNROLL]:
             if step > 0:
-                peer = lax.rem(me + step, bins)
-                peer_copy(step, rounded.at[peer], mixed.at[me], mix_send, mix_recv).start()
+                peer = lax.rem(me + turned(step), bins)
+                peer_copy(turned(step), rounded.at[peer], mixed.at[me], mix_send, mix_recv).start()
     mixed[me] = rounded[me]
     for step in range(1, bins):
         peer_arrived(step, rounded.at[0], mixed, mix_send, mix_recv)
@@ -320,8 +325,8 @@
     change = gain - loss.astype(jnp.float32)
     delta[...] = change.astype(jnp.bfloat16).reshape(bins, rows, LANES)
     for step in order[:-1]:
-        peer = lax.rem(me + step, bins)
-        peer_copy(step, delta.at[peer], back.at[me], back_send, back_recv).start()
+        peer = lax.rem(me + turned(step), bins)
+        peer_copy(turned(step), delta.at[peer], back.at[me], back_send, back_recv).start()
     back[me] = delta[me]
     for step in range(1, bins):
         peer_arrived(step, delta.at[0], back, back_send, back_recv)

time: 33.3 us -> 33.3 us (level)
  no operation moved by 1% of the time
where the time goes in v7:
time: 33.3 us; the launch traced here: 33.2 us
  Pallas kernels  32.6 us (98%)
  between operations  0.64 us (2%)
    pallas_call x1, Pallas kernels, body(): pl.pallas_call(run, name='dust_step', out_shape=tuple((pltpu.VMEM(shape,...  31.9 us
    pallas_call x1, Pallas kernels, body(): pl.pallas_call(store_body, name='dust_store', out_shape=tuple((jax.ShapeD...  0.71 us

profile of v7, /device:TPU:4, one launch (start us, length us, event | category | flops | bytes accessed | tf_op | source)
XLA Modules:
  0.0 33.2 jit_solution(16540744567029782198)
XLA Ops:
  0.6 31.9 %dust_step.1 = (f32[16,1024]{1,0:T(8,128)S(1)}, f32[2,16,1024]{2,1,0:T(8,128)S(1)}, f32[2,1024]{1,0:T(2,128)S(1)}) custom-call(f32[16,1024]{1,0:T(8,128)} %refs_0_.1, f32[2,16,1024]{2,1,0:T(8,128)} %refs_1_.1, f32[8,128]{1,0:T(8,128)} %bitcast.5, f32[2,1024]{1,0:T(2,128)} %refs_3_.1, f32[2,8,1024]{2,1,0:T(8,128)} %refs_4_.1, f32[8,128]{1,0:T(8,128)} %bitcast.6, ...), custom_call_target="tpu_custom_call" | custom-call | tf_op jit(solution)/shard_map/dust_step/pallas_call | solution.py:399
  32.5 0.7 %dust_store.1 = (f32[16,1024]{1,0:T(8,128)}, f32[2,16,1024]{2,1,0:T(8,128)}, f32[2,1024]{1,0:T(2,128)}) custom-call(f32[16,1024]{1,0:T(8,128)S(1)} %get-tuple-element.6.rho, f32[2,16,1024]{2,1,0:T(8,128)S(1)} %get-tuple-element.7.vel, f32[2,1024]{1,0:T(2,128)S(1)} %get-tuple-element.8.gas), custom_call_target="tpu_custom_call" | custom-call | tf_op jit(solution)/shard_map/dust_store/pallas_call | solution.py:438
